TPU v7x, 32 devices: a whole 2x2x4 slice. The times are simulated.
32 devices in a mesh: row: 4 (over z), bulk: 8 (over y, x, core).
Axes of the slice: x: 2, y: 2, z: 4, core: 2. Of those that a mesh axis runs over, the one named last changes fastest.
Arguments:
- child_inverse: float32 [2, 4096, 4096], P(None, 'row', 'bulk')
- child_rhs: float32 [2, 4096, 256], P(None, 'bulk'), may hold values from -6 to 6
- child_update: float32 [2, 1024, 4096], P(None, 'bulk', 'row'), may hold values from -0.09375 to 0.09375
- targets: int32 [2, 1024], replicated, may hold values from 0 to 8191, as said below
- root_inverse: float32 [8192, 8192], P('row', 'bulk')
- root_rhs: float32 [8192, 256], P('bulk'), may hold values from -6 to 6
Outputs:
- root_solution: float32 [8192, 256], P('bulk')
- child_solution: float32 [2, 4096, 256], P(None, 'bulk')
Inputs may be any that keep to these rules, and one draw needn't show every extreme that they name: `targets`: for each child, the 128 update rows k * 128 to (k + 1) * 128 - 1 name at most 32 rows of one owner, the owner of root row t being t // 1024; in every such block some owner is named exactly 32 times. A root row may be named more than once.
All inputs are finite; a program needn't handle non-finite values.
Results may differ from a plain program's by a relative error of at most 0.00007.
Values sent between devices are 32-bit elements; how exact they have to be, the bound alone decides.
A program may use at most 128 MiB of HBM per device.

v0:
```python
import jax
import jax.numpy as jnp
from jax import lax
from jax.sharding import PartitionSpec as P

highest = lax.Precision.HIGHEST


def slot_map(own_targets, owned_rows, owner_count, capacity):
    destination = own_targets // owned_rows
    owner_hits = (destination[:, :, None] == jnp.arange(owner_count)[None, None, :]).astype(
        jnp.int32
    )
    earlier = jnp.cumsum(owner_hits, axis=1) - owner_hits
    placement = jnp.sum(earlier * owner_hits, axis=2)
    slot_index = destination * capacity + placement
    return (jnp.arange(owner_count * capacity)[None, :, None] == slot_index[:, None, :]).astype(
        jnp.float32
    )


def receive_map(targets, owner_index, owned_rows, owner_count, local_rows, capacity):
    every_target = targets.reshape(2, owner_count, local_rows)
    arriving = (every_target // owned_rows == owner_index).astype(jnp.int32)
    earlier = jnp.cumsum(arriving, axis=2) - arriving
    offsets = every_target - owner_index * owned_rows
    matching = (arriving[..., None] == 1) & (
        earlier[..., None] == jnp.arange(capacity)[None, None, None, :]
    )
    slot_offset = jnp.sum(jnp.where(matching, offsets[..., None], 0), axis=2)
    slot_valid = jnp.any(matching, axis=2)
    placing = (
        jnp.arange(owned_rows)[:, None] == slot_offset.reshape(-1)[None, :]
    ) & slot_valid.reshape(-1)[None, :]
    return placing.astype(jnp.float32)


def per_device(child_inverse, child_rhs, child_update, targets, root_inverse, root_rhs):
    owner_index = lax.axis_index("bulk")
    owner_count = lax.axis_size("bulk")
    local_rows = child_update.shape[1]
    owned_rows = root_rhs.shape[0]
    capacity = max(2, 2 * local_rows // owner_count)
    child_partial = jnp.einsum("jab,jbr->jar", child_inverse, child_rhs, precision=highest)
    forward_child = lax.psum(child_partial, "bulk")
    update_partial = jnp.einsum("jua,jar->jur", child_update, forward_child, precision=highest)
    updates = lax.psum(update_partial, "row")
    share_columns = updates.shape[2]
    own_targets = lax.dynamic_slice_in_dim(targets, owner_index * local_rows, local_rows, 1)
    sending = slot_map(own_targets, owned_rows, owner_count, capacity)
    outgoing = jnp.einsum("jsu,jur->jsr", sending, updates, precision=highest)
    outgoing = outgoing.reshape(2, owner_count, capacity, share_columns)
    incoming = lax.all_to_all(outgoing, "bulk", split_axis=1, concat_axis=1, tiled=True)
    placing = receive_map(targets, owner_index, owned_rows, owner_count, local_rows, capacity)
    assembled = jnp.dot(placing, incoming.reshape(-1, share_columns), precision=highest)
    root_partial = jnp.dot(root_inverse, root_rhs - assembled, precision=highest)
    forward_root = lax.psum(root_partial, "bulk")
    back_partial = jnp.einsum("ab,ar->br", root_inverse, forward_root, precision=highest)
    root_solution = lax.psum(back_partial, "row")
    reply = jnp.einsum("tc,tr->cr", placing, root_solution, precision=highest)
    reply = reply.reshape(2, owner_count, capacity, share_columns)
    returned = lax.all_to_all(reply, "bulk", split_axis=1, concat_axis=1, tiled=True)
    fetched = jnp.einsum(
        "jsu,jsr->jur",
        sending,
        returned.reshape(2, owner_count * capacity, share_columns),
        precision=highest,
    )
    coupling_partial = jnp.einsum("jua,jur->jar", child_update, fetched, precision=highest)
    coupling = lax.psum(coupling_partial, "bulk")
    child_partial_back = jnp.einsum(
        "jab,jar->jbr", child_inverse, forward_child - coupling, precision=highest
    )
    child_solution = lax.psum(child_partial_back, "row")
    return (root_solution, child_solution)


def solution(mesh):
    return jax.shard_map(
        per_device,
        mesh=mesh,
        in_specs=(
            P(None, "row", "bulk"),
            P(None, "bulk", None),
            P(None, "bulk", "row"),
            P(),
            P("row", "bulk"),
            P("bulk", None),
        ),
        out_specs=(P("bulk", None), P(None, "bulk", None)),
        check_vma=False,
    )
```

profile of v0, /device:TPU:0, one launch (start us, length us, event | category | flops | bytes accessed | tf_op | source)
XLA Modules:
  0.0 422.1 jit_solution(4172962893462993971)
XLA Ops:
  7.2 7.5 %fusion.33 = f32[2,1024,256]{2,1,0:T(8,128)} fusion(f32[2,1024,512]{2,1,0:T(8,128)} %param.6, f32[2,512,256]{2,1,0:T(8,128)} %param.7), kind=kOutput, calls=%fused_computation.48 | convolution fusion | flops 3221225472 | bytes 7340032 | tf_op jit(solution)/shard_map/jab,jbr->jar/dot_general | solution.py:44
  14.8 0.6 copy-done.3
  15.8 63.3 %all-reduce.7.cloned.1.call-done = f32[2,1024,256]{2,1,0:T(8,128)} async-done(((f32[2,1024,256]{2,1,0:T(8,128)}), f32[2,1024,256]{2,1,0:T(8,128)}) %all-reduce.7.cloned.1.call-update) | async-done | bytes 2097168 | tf_op jit(solution)/shard_map/psum | solution.py:45
  79.0 5.8 %convolution_bitcast_fusion.3 = f32[2,128,256]{1,2,0:T(8,128)} fusion(f32[2,1024,256]{2,1,0:T(8,128)} %all-reduce.7.cloned.1.call-done, f32[2,128,1024]{2,1,0:T(8,128)S(1)} %copy-done), kind=kOutput, calls=%fused_computation.11 | convolution fusion | flops 805306368 | bytes 3407872 | tf_op jit(solution)/shard_map/jua,jar->jur/dot_general | solution.py:46
  85.0 0.6 reduce_window_sum.22
  85.6 33.9 %all-reduce.9.cloned.1.call-done = f32[2,128,256]{1,2,0:T(8,128)} async-done(((f32[2,128,256]{1,2,0:T(8,128)}), f32[2,128,256]{1,2,0:T(8,128)}) %all-reduce.9.cloned.1.call-update) | async-done | bytes 262160 | tf_op jit(solution)/shard_map/psum | solution.py:47
  119.5 1.4 fusion.22
  120.9 0.8 copy.31
  121.8 3.6 all-to-all-start
  126.5 8.6 %all-to-all-done = f32[2,8,32,256]{3,2,0,1:T(8,128)S(1)} async-done(((f32[2,8,32,256]{3,2,0,1:T(8,128)}), f32[2,8,32,256]{3,2,0,1:T(8,128)S(1)}, u32[]{:S(2)}, u32[]{:S(2)}) %all-to-all-start) | async-done | bytes 524320 | tf_op jit(solution)/shard_map/all_to_all | solution.py:53
  135.2 1.2 fusion.6
  136.4 16.8 %convolution_bitcast_fusion = f32[2048,256]{0,1:T(8,128)} fusion(f32[1024,256]{1,0:T(8,128)S(1)} %fusion.6, f32[2048,1024]{1,0:T(8,128)} %param.10), kind=kOutput, calls=%fused_computation | convolution fusion | flops 6442450944 | bytes 11534336 | tf_op jit(solution)/shard_map/dot_general | solution.py:56
  153.3 59.5 %all-reduce.11.cloned.1.call-done = f32[2048,256]{0,1:T(8,128)} async-done(((f32[2048,256]{0,1:T(8,128)}), f32[2048,256]{0,1:T(8,128)}) %all-reduce.11.cloned.1.call-update) | async-done | bytes 2097168 | tf_op jit(solution)/shard_map/psum | solution.py:57
  212.7 11.0 %convolution_bitcast_fusion.2 = f32[1024,256]{0,1:T(8,128)} fusion(f32[2048,256]{0,1:T(8,128)} %all-reduce.11.cloned.1.call-done, f32[2048,1024]{1,0:T(8,128)} %param.10), kind=kOutput, calls=%fused_computation.10 | convolution fusion | flops 6442450944 | bytes 11534336 | tf_op jit(solution)/shard_map/ab,ar->br/dot_general | solution.py:58
  224.1 50.9 %all-reduce.13.cloned.1.call-done = f32[1024,256]{0,1:T(8,128)} async-done(((f32[1024,256]{0,1:T(8,128)}), f32[1024,256]{0,1:T(8,128)}) %all-reduce.13.cloned.1.call-update) | async-done | bytes 1048592 | tf_op jit(solution)/shard_map/psum | solution.py:59
  275.0 2.7 fusion.12
  277.7 13.2 %all_to_all.10 = f32[2,8,32,256]{3,2,0,1:T(8,128)S(1)} all-to-all(f32[2,8,32,256]{3,2,0,1:T(8,128)S(1)} %copy.33), channel_id=1, replica_groups=mesh['row'=4,'bulk'=8] {'bulk'}, dimensions={1} | all-to-all | bytes 1048576 | tf_op jit(solution)/shard_map/all_to_all | solution.py:62
  291.0 0.7 fusion.18
  291.7 3.2 convolution_bitcast_fusion.1
  294.9 59.1 %all-reduce.15.cloned.1.call-done = f32[2,1024,256]{2,1,0:T(8,128)} async-done(((f32[2,1024,256]{2,1,0:T(8,128)}), f32[2,1024,256]{2,1,0:T(8,128)}) %all-reduce.15.cloned.1.call-update) | async-done | bytes 2097168 | tf_op jit(solution)/shard_map/psum | solution.py:70
  354.1 7.5 %fusion.9 = f32[2,512,256]{1,2,0:T(8,128)} fusion(f32[2,1024,512]{2,1,0:T(8,128)} %param.6, f32[2,1024,256]{2,1,0:T(8,128)S(1)} %copy-done.1, f32[2,1024,256]{2,1,0:T(8,128)} %all-reduce.15.cloned.1.call-done), kind=kOutput, calls=%fused_computation.9 | convolution fusion | flops 3221749760 | bytes 9437184 | tf_op jit(solution)/shard_map/jab,jar->jbr/dot_general | solution.py:71
  361.6 2.5 copy.38
  364.1 48.6 %all-reduce.17.cloned.1.call-done = f32[2,512,256]{1,2,0:T(8,128)} async-done(((f32[2,512,256]{1,2,0:T(8,128)}), f32[2,512,256]{1,2,0:T(8,128)}) %all-reduce.17.cloned.1.call-update) | async-done | bytes 1048592 | tf_op jit(solution)/shard_map/psum | solution.py:74
  412.8 2.5 copy.39
  (34 shorter events, 2.3 us)
Async XLA Ops:
  7.2 71.9 %copy-start = (f32[2,128,1024]{2,1,0:T(8,128)S(1)}, f32[2,128,1024]{2,1,0:T(8,128)}, u32[]{:S(2)}) copy-start(f32[2,128,1024]{2,1,0:T(8,128)} %param.8) | copy-start | bytes 3145732
  7.2 71.9 %all-reduce.7.cloned.1.call-start = ((), (), s32[]{:S(2)}) async-start(), calls=%async_computation.2 | async-start | bytes 4194304 | tf_op jit(solution)/shard_map/psum | solution.py:45
  14.7 0.7 copy-start.3
  14.8 104.7 %all-reduce.9.cloned.1.call-start = ((), (), s32[]{:S(2)}) async-start(), calls=%async_computation.3 | async-start | bytes 524288 | tf_op jit(solution)/shard_map/psum | solution.py:47
  84.8 50.4 %copy-start.2 = (f32[1024,256]{1,0:T(8,128)S(1)}, f32[1024,256]{1,0:T(8,128)}, u32[]{:S(2)}) copy-start(f32[1024,256]{1,0:T(8,128)} %param.11) | copy-start | bytes 3145732
  121.8 13.4 %all-to-all-start = ((f32[2,8,32,256]{3,2,0,1:T(8,128)}), f32[2,8,32,256]{3,2,0,1:T(8,128)S(1)}, u32[]{:S(2)}, u32[]{:S(2)}) async-start(f32[2,8,32,256]{3,2,0,1:T(8,128)} %copy.31), calls=%async_computation | async-start | bytes 1048576 | tf_op jit(solution)/shard_map/all_to_all | solution.py:53
  125.4 87.3 %all-reduce.11.cloned.1.call-start = ((), (), s32[]{:S(2)}) async-start(), calls=%async_computation.4 | async-start | bytes 4194304 | tf_op jit(solution)/shard_map/psum | solution.py:57
  153.2 121.7 %all-reduce.13.cloned.1.call-start = ((), (), s32[]{:S(2)}) async-start(), calls=%async_computation.5 | async-start | bytes 2097152 | tf_op jit(solution)/shard_map/psum | solution.py:59
  223.8 130.2 %all-reduce.15.cloned.1.call-start = ((), (), s32[]{:S(2)}) async-start(), calls=%async_computation.6 | async-start | bytes 4194304 | tf_op jit(solution)/shard_map/psum | solution.py:70
  291.7 62.4 %copy-start.1 = (f32[2,1024,256]{2,1,0:T(8,128)S(1)}, f32[2,1024,256]{2,1,0:T(8,128)}, u32[]{:S(2)}) copy-start(f32[2,1024,256]{2,1,0:T(8,128)} %all-reduce.7.cloned.1.call-done) | copy-start | bytes 6291460
  294.9 117.9 %all-reduce.17.cloned.1.call-start = ((), (), s32[]{:S(2)}) async-start(), calls=%async_computation.7 | async-start | bytes 2097152 | tf_op jit(solution)/shard_map/psum | solution.py:74
Sparse Core Ops, SparseCore 0:
  14.9 64.0 all-reduce.6
  84.9 34.5 all-reduce.8
  153.4 59.3 all-reduce.10
  223.9 51.0 all-reduce.12
  295.0 59.0 all-reduce.14
  361.7 50.9 all-reduce.16
where the time goes:
time: 423 us; the launch traced here: 422 us
  waiting for transfers between devices  324 us (77%)
  matrix products  57.8 us (14%)
  between operations  14.2 us (3%)
  blocking collectives  13.2 us (3%)
  local copies, waits for them, and re-layouts  6.81 us (2%)
  starting transfers between devices  4.29 us (1%)
    psum x1, waiting for transfers between devices, per_device(): forward_child = lax.psum(child_partial, 'bulk')  63.3 us
    psum x1, waiting for transfers between devices, per_device(): forward_root = lax.psum(root_partial, 'bulk')  59.5 us
    psum x1, waiting for transfers between devices, per_device(): coupling = lax.psum(coupling_partial, 'bulk')  59.1 us
    psum x1, waiting for transfers between devices, per_device(): root_solution = lax.psum(back_partial, 'row')  50.9 us
    psum x1, waiting for transfers between devices, per_device(): child_solution = lax.psum(child_partial_back, 'row')  48.6 us
    psum x1, waiting for transfers between devices, per_device(): updates = lax.psum(update_partial, 'row')  33.9 us
    dot_general x1, matrix products, per_device(): jnp.dot(root_inverse, root_rhs - assembled, precision=highest)  16.8 us
    all_to_all x1, blocking collectives, per_device(): lax.all_to_all(reply, 'bulk', split_axis=1, concat_axis=1, tiled=True)  13.2 us
  transfers between devices with their start and end apart: 7, of which 7 were waited for; matrix products, arithmetic and copies ran while one was open for 1% of the time, Pallas kernels for 0%

commit v1 on v0

v1 whole, which is shorter than its diff:
```python
import functools

import jax
import jax.numpy as jnp
from jax import lax
from jax.experimental import pallas as pl
from jax.experimental.pallas import tpu as pltpu
from jax.sharding import PartitionSpec as P

MESH = pl.DeviceIdType.MESH
CHUNKS = 2
OFFSET = 3
f32, bf16 = jnp.float32, jnp.bfloat16


def split(x):
    high = x.astype(bf16)
    return high, (x - high.astype(f32)).astype(bf16)


def bit_orders(bits):
    rest = list(range(1, bits))
    return ([0] + rest, [0] + rest[::-1])


def block_position(block, order, bits):
    position = 0
    for step, bit in enumerate(order):
        position += ((block >> bit) & 1) << (bits - 1 - step)
    return position


def dot(a, b):
    return jnp.dot(a, b, preferred_element_type=f32)


def kernel(
    nb, nr, dims,
    ci_hbm, crhs_ref, cu_hbm, trow_ref, tcol_ref, ri_hbm, rrhs_ref,
    root_out, child_out,
    ci, cu, ri,
    part, fcr, fc, ug, frp, frr, fr, rep, repr_, cp, cpr,
    up, upx, bk, bkx, cb, cbx,
    rhs_w, tmp_t,
    load_sem, ar_s, ar_r, ch_s, ch_r,
):
    bits = nb.bit_length() - 1
    orders = bit_orders(bits)
    me = lax.axis_index("bulk")
    row = lax.axis_index("row")
    C = fc.shape[-1]
    cols_a, cols_b, own, rows_a, nl = dims

    loads = [
        pltpu.make_async_copy(ci_hbm, ci, load_sem.at[0]),
        pltpu.make_async_copy(cu_hbm, cu, load_sem.at[1]),
        pltpu.make_async_copy(ri_hbm, ri, load_sem.at[2]),
    ]
    for load in loads:
        load.start()

    def partner_of(bit):
        size = 1 << bit
        mine = (me // size) % 2
        return mine, me + size * (1 - 2 * mine)

    right = lax.rem(row + 1, nr)
    left = lax.rem(row + nr - 1, nr)
    barrier = pltpu.get_barrier_semaphore()
    for bit in range(bits):
        pl.semaphore_signal(barrier, inc=1, device_id={"bulk": partner_of(bit)[1]}, device_id_type=MESH)

    for side in (left, right):
        pl.semaphore_signal(barrier, inc=1, device_id={"row": side}, device_id_type=MESH)
    pl.semaphore_wait(barrier, bits + 2)

    def remote(src, dst, send, recv, **where):
        return pltpu.make_async_remote_copy(
            src_ref=src, dst_ref=dst, send_sem=send, recv_sem=recv, device_id=where, device_id_type=MESH
        )

    def reduce_scatter(h, which, buf, rbuf, starts, out):
        n = buf.shape[2]
        length, off, sends = n, 0, []
        for step in range(bits):
            half = length // 2
            flights = []
            for f in range(2):
                mine, partner = partner_of(orders[f][step])
                away = pl.multiple_of(starts[f] + (1 - mine) * half, half)
                keep = pl.multiple_of(starts[f] + mine * half, half)
                copy = remote(
                    buf.at[h, f, pl.ds(away, half)], rbuf.at[h, f, pl.ds(off, half)],
                    ar_s.at[h, which, f, step], ar_r.at[h, which, f, step], bulk=partner,
                )
                copy.start()
                flights.append((copy, keep))
            yield
            for f, (copy, keep) in enumerate(flights):
                copy.wait_recv()
                target = out if step == bits - 1 else buf
                target[h, f, pl.ds(keep, half)] = buf[h, f, pl.ds(keep, half)] + rbuf[h, f, pl.ds(off, half)]
                starts[f] = keep
                sends.append(copy)
            length, off = half, off + half
        for copy in sends:
            copy.wait_send()

    def all_gather(h, which, buf, starts):
        n = buf.shape[2]
        for step in reversed(range(bits)):
            length = n >> (step + 1)
            flights = []
            for f in range(2):
                mine, partner = partner_of(orders[f][step])
                here = buf.at[h, f, pl.ds(pl.multiple_of(starts[f], length), length)]
                copy = remote(
                    here, here, ar_s.at[h, which, f, step], ar_r.at[h, which, f, step], bulk=partner
                )
                copy.start()
                flights.append((copy, mine))
            yield
            for f, (copy, mine) in enumerate(flights):
                copy.wait_send()
                copy.wait_recv()
                starts[f] = starts[f] - mine * length

    def chain(h, which, p, x):
        pieces = p.shape[1]

        @pl.when(row == 0)
        def _():
            x[h, 0] = jnp.zeros(x.shape[2:], f32)

        @pl.when(row == nr - 1)
        def _():
            x[h, 1] = jnp.zeros(x.shape[2:], f32)

        def flow(side, i, has_source, has_target, target):
            copy = remote(
                x.at[h, 2 + side, i], x.at[h, side, i],
                ch_s.at[h, which, side, i], ch_r.at[h, which, side, i], row=target,
            )

            @pl.when(has_source)
            def _():
                copy.wait_recv()

            @pl.when(has_target)
            def _():
                x[h, 2 + side, i] = x[h, side, i] + p[h, i]
                copy.start()

        for t in range(pieces + nr - 1):
            if t > 0:
                yield
            i = t - row

            @pl.when((i >= 0) & (i < pieces))
            def _():
                flow(0, i, row > 0, row < nr - 1, right)

            k = t - (nr - 1 - row)

            @pl.when((k >= 0) & (k < pieces))
            def _():
                flow(1, k, row < nr - 1, row > 0, left)

        for i in range(pieces):
            for side, has_target, target in ((0, row < nr - 1, right), (1, row > 0, left)):
                @pl.when(has_target)
                def _():
                    remote(
                        x.at[h, 2 + side, i], x.at[h, side, i],
                        ch_s.at[h, which, side, i], ch_r.at[h, which, side, i], row=target,
                    ).wait_send()

    def times(a_tile, count, store, h, width):
        def body(i, carry):
            high, low = split(a_tile(i))
            both = dot(high, rhs_w[h, :width]) + dot(low, rhs_w[h, :width])
            store(i, both[:, :C] + both[:, C:])
            return carry

        lax.fori_loop(0, count, body, 0)

    def keep_right(h, at, value):
        high, low = split(value)
        rhs_w[h, at, :C] = high
        rhs_w[h, at, C:] = low

    def transposed_times(a_tile, depth, k_tile, y_tile, count, width, store, h):
        for k in range(depth // k_tile):
            high, low = split(y_tile(k).T)
            tmp_t[h, :C, k * k_tile:(k + 1) * k_tile] = high
            tmp_t[h, C:, k * k_tile:(k + 1) * k_tile] = low

        def body(i, carry):
            total = jnp.zeros((2 * C, width), f32)
            for k in range(depth // k_tile):
                high, low = split(a_tile(k, i))
                y = tmp_t[h, :, k * k_tile:(k + 1) * k_tile]
                total += dot(y, high) + dot(y, low)
            store(i, (total[:C] + total[C:]).T)
            return carry

        lax.fori_loop(0, count, body, 0)

    def tiles(n, most):
        size = min(n, most)
        return size, n // size

    def program(h):
        lanes = slice(h * C, (h + 1) * C)
        if h == 0:
            loads[0].wait()
        tm, count = tiles(cols_a, 256)
        for j in range(2):
            keep_right(h, slice(0, cols_b), crhs_ref[j, :, lanes])

            def store(i, value, j=j):
                part[h, j, pl.ds(pl.multiple_of(i * tm, tm), tm)] = value

            times(lambda i, j=j: ci[j, pl.ds(pl.multiple_of(i * tm, tm), tm), :], count, store, h, cols_b)
        starts = [0, 0]
        yield from reduce_scatter(h, 0, part, fcr, starts, fc)
        yield from all_gather(h, 1, fc, starts)
        if h == 0:
            loads[1].wait()
        for j in range(2):
            keep_right(h, slice(0, cols_a), fc[h, j])

            def store(i, value, j=j):
                up[h, j] = value

            times(lambda i, j=j: cu[j], 1, store, h, cols_a)
        yield from chain(h, 0, up, upx)
        starts = []
        for j in range(2):
            position = 0
            for step, bit in enumerate(orders[j]):
                position = position + ((me // (1 << bit)) % 2) * (1 << (bits - 1 - step))
            start = pl.multiple_of(position * nl, nl)
            starts.append(start)
            ug[h, j, pl.ds(start, nl)] = upx[h, 0, j] + up[h, j] + upx[h, 1, j]
        yield from all_gather(h, 2, ug, starts)
        tm, count = tiles(own, 256)
        nu = nb * nl
        kt, kcount = tiles(nu, 512)

        def assemble(i, carry):
            ids = lax.broadcasted_iota(jnp.int32, (tm, kt), 0) + (me * own + i * tm)
            at = pl.ds(pl.multiple_of(i * tm, tm), tm)
            total = jnp.zeros((tm, C), f32)
            for j in range(2):
                for k in range(kcount):
                    ks = slice(k * kt, (k + 1) * kt)
                    hit = jnp.where(ids == trow_ref[j:j + 1, ks], 1.0, 0.0).astype(bf16)
                    high, low = split(ug[h, j, ks])
                    total += dot(hit, high) + dot(hit, low)
            value = rrhs_ref[at, lanes] - total
            high, low = split(value)
            rhs_w[h, at, :C] = high
            rhs_w[h, at, C:] = low
            return carry

        lax.fori_loop(0, count, assemble, 0)
        if h == 0:
            loads[2].wait()
        per = rows_a // 2
        tm4, count4 = tiles(per, 256)
        for f in range(2):
            def store(i, value, f=f):
                frp[h, f, pl.ds(pl.multiple_of(i * tm4, tm4), tm4)] = value

            times(
                lambda i, f=f: ri[pl.ds(pl.multiple_of(f * per + i * tm4, tm4), tm4), :],
                count4, store, h, own,
            )
        starts = [0, 0]
        yield from reduce_scatter(h, 3, frp, frr, starts, fr)
        yield from all_gather(h, 4, fr, starts)
        pieces, size = bk.shape[1], bk.shape[2]
        width = min(256, own)
        kt5, _ = tiles(per, 512)
        halves = per // kt5

        def store(i, value):
            for s in range(max(1, width // size)):
                piece = min(width, size)
                if size >= width:
                    each = size // width
                    bk[h, i // each, pl.ds(pl.multiple_of((i % each) * width, width), width)] = value
                else:
                    bk[h, i * (width // size) + s] = value[s * piece:(s + 1) * piece]

        transposed_times(
            lambda k, i: ri[k * kt5:(k + 1) * kt5, pl.ds(pl.multiple_of(i * width, width), width)],
            rows_a, kt5,
            lambda k: fr[h, k // halves, (k % halves) * kt5:(k % halves + 1) * kt5],
            own // width, width, store, h,
        )
        yield from chain(h, 1, bk, bkx)
        for i in range(pieces):
            value = bkx[h, 0, i] + bk[h, i] + bkx[h, 1, i]
            root_out[i * size:(i + 1) * size, lanes] = value
            keep_right(h, slice(i * size, (i + 1) * size), value)
        tm6, count6 = tiles(nu, 256)
        for j in range(2):
            def fetch(i, carry, j=j):
                at = pl.ds(pl.multiple_of(i * tm6, tm6), tm6)
                ids = lax.broadcasted_iota(jnp.int32, (tm6, own), 1) + me * own
                hit = jnp.where(ids == tcol_ref[j, at], 1.0, 0.0).astype(bf16)
                both = dot(hit, rhs_w[h, :own])
                rep[h, j, at] = both[:, :C] + both[:, C:]
                return carry

            lax.fori_loop(0, count6, fetch, 0)
        starts = [0, 0]
        yield from reduce_scatter(h, 5, rep, repr_, starts, rep)
        w7, count7 = tiles(cols_a, 256)
        for j in range(2):
            def store(i, value, j=j):
                cp[h, j, pl.ds(pl.multiple_of(i * w7, w7), w7)] = value

            transposed_times(
                lambda k, i, j=j: cu[j, :, pl.ds(pl.multiple_of(i * w7, w7), w7)],
                nl, nl,
                lambda k, j=j: rep[h, j, pl.ds(starts[j], nl)],
                count7, w7, store, h,
            )
        starts7 = [0, 0]
        yield from reduce_scatter(h, 6, cp, cpr, starts7, part)
        yield from all_gather(h, 7, part, starts7)
        pieces8, size8 = cb.shape[1], cb.shape[2]
        w8, count8 = tiles(cols_b, size8)
        kt8, _ = tiles(cols_a, 512)
        for j in range(2):
            def store(i, value, j=j):
                cb[h, j * (pieces8 // 2) + i] = value

            transposed_times(
                lambda k, i, j=j: ci[j, k * kt8:(k + 1) * kt8, pl.ds(pl.multiple_of(i * w8, w8), w8)],
                cols_a, kt8,
                lambda k, j=j: fc[h, j, k * kt8:(k + 1) * kt8] - part[h, j, k * kt8:(k + 1) * kt8],
                count8, w8, store, h,
            )
        yield from chain(h, 2, cb, cbx)
        for i in range(pieces8):
            j, k = i // (pieces8 // 2), i % (pieces8 // 2)
            child_out[j, k * size8:(k + 1) * size8, lanes] = cbx[h, 0, i] + cb[h, i] + cbx[h, 1, i]

    running = [program(h) for h in range(CHUNKS)]
    turn = 0
    while any(p is not None for p in running):
        for h in range(CHUNKS):
            if running[h] is not None and turn >= h * OFFSET:
                try:
                    next(running[h])
                except StopIteration:
                    running[h] = None
        turn += 1


def per_device(nb, nr, child_inverse, child_rhs, child_update, targets, root_inverse, root_rhs):
    bits = nb.bit_length() - 1
    orders = bit_orders(bits)
    _, cols_a, cols_b = child_inverse.shape
    nl = child_update.shape[1]
    rows_a, own = root_inverse.shape
    R = root_rhs.shape[1]
    H, C = CHUNKS, R // CHUNKS
    nu = nb * nl
    blocks = targets.reshape(2, nb, nl)
    placed = []
    for j in range(2):
        source = [0] * nb
        for block in range(nb):
            source[block_position(block, orders[j], bits)] = block
        placed.append(jnp.concatenate([blocks[j, s] for s in source]))
    trow = jnp.stack(placed)
    tcol = trow[:, :, None]
    root_pieces = max(1, min(4, own // 128))
    child_pieces = 2 * max(1, min(2, cols_b // 128))
    most = max(root_pieces, child_pieces, 2)
    any_, vmem = pl.BlockSpec(memory_space=pl.ANY), pl.BlockSpec(memory_space=pltpu.VMEM)

    def sums(n, count=2):
        return [pltpu.VMEM((H, 2, n, C), f32)] * count

    def chains(pieces, rows):
        return [pltpu.VMEM((H, pieces, rows, C), f32), pltpu.VMEM((H, 4, pieces, rows, C), f32)]

    return pl.pallas_call(
        functools.partial(kernel, nb, nr, (cols_a, cols_b, own, rows_a, nl)),
        out_shape=(
            jax.ShapeDtypeStruct(root_rhs.shape, f32),
            jax.ShapeDtypeStruct(child_rhs.shape, f32),
        ),
        in_specs=[any_, vmem, any_, vmem, vmem, any_, vmem],
        out_specs=(vmem, vmem),
        scratch_shapes=[
            pltpu.VMEM(child_inverse.shape, f32),
            pltpu.VMEM(child_update.shape, f32),
            pltpu.VMEM(root_inverse.shape, f32),
            *sums(cols_a, 3),
            pltpu.VMEM((H, 2, nu, C), f32),
            *sums(rows_a // 2, 3),
            *sums(nu),
            *sums(cols_a),
            *chains(2, nl),
            *chains(root_pieces, own // root_pieces),
            *chains(child_pieces, 2 * cols_b // child_pieces),
            pltpu.VMEM((H, max(own, cols_a, cols_b), 2 * C), bf16),
            pltpu.VMEM((H, 2 * C, max(rows_a, cols_a, nl)), bf16),
            pltpu.SemaphoreType.DMA((3,)),
            pltpu.SemaphoreType.DMA((H, 8, 2, bits)),
            pltpu.SemaphoreType.DMA((H, 8, 2, bits)),
            pltpu.SemaphoreType.DMA((H, 3, 2, most)),
            pltpu.SemaphoreType.DMA((H, 3, 2, most)),
        ],
        compiler_params=pltpu.CompilerParams(
            collective_id=0, has_side_effects=True, vmem_limit_bytes=62 * 1024 * 1024
        ),
    )(child_inverse, child_rhs, child_update, trow, tcol, root_inverse, root_rhs)


def solution(mesh):
    return jax.shard_map(
        functools.partial(per_device, mesh.shape["bulk"], mesh.shape["row"]),
        mesh=mesh,
        in_specs=(
            P(None, "row", "bulk"),
            P(None, "bulk", None),
            P(None, "bulk", "row"),
            P(),
            P("row", "bulk"),
            P("bulk", None),
        ),
        out_specs=(P("bulk", None), P(None, "bulk", None)),
        check_vma=False,
    )
```

time: 423 us -> 214 us (0.51)
  waiting for transfers between devices: 324 us -> 0 us
  Pallas kernels: 0 us -> 206 us
  matrix products: 57.8 us -> 0 us
  between operations: 14.2 us -> 0.7 us
  blocking collectives: 13.2 us -> 0 us
  starting transfers between devices: 4.29 us -> 0 us
    psum x6 -> x0, waiting for transfers between devices: 315 us -> none  [the longest x1 63.3 us: per_device(): forward_child = lax.psum(child_partial, 'bulk')]
    pallas_call x0 -> x1, Pallas kernels: none -> 206 us  [per_device(): pl.pallas_call(functools.partial(kernel, nb, nr, (cols_a, cols_b, own, ro...]
    dot_general x10 -> x0, matrix products: 57.8 us -> none  [the longest x1 16.8 us: per_device(): jnp.dot(root_inverse, root_rhs - assembled, precision=highest)]
    all_to_all x1 -> x0, blocking collectives: 13.2 us -> none  [per_device(): lax.all_to_all(reply, 'bulk', split_axis=1, concat_axis=1, tiled=True)]
    all_to_all x1 -> x0, waiting for transfers between devices: 8.62 us -> none  [per_device(): lax.all_to_all(outgoing, 'bulk', split_axis=1, concat_axis=1, tiled=True)]
  transfers between devices with their start and end apart: 7 -> 0, of which waited for: 7 -> 0; matrix products, arithmetic and copies ran while one was open for 1% -> 0% of each run, Pallas kernels for 0% -> 0%
where the time goes in v1:
time: 214 us
  Pallas kernels  206 us (96%)
  local copies, waits for them, and re-layouts  6.63 us (3%)
    pallas_call x1, Pallas kernels, per_device(): pl.pallas_call(functools.partial(kernel, nb, nr, (cols_a, cols_b, own, ro...  206 us
    unnamed x10, local copies, waits for them, and re-layouts  5.28 us

profile of v1, /device:TPU:0, one launch (start us, length us, event | category | flops | bytes accessed | tf_op | source)
XLA Modules:
  0.0 213.5 jit_solution(1988453382002542565)
XLA Ops:
  0.6 0.7 copy.11
  1.5 0.6 fusion
  2.1 1.3 copy.8.tcol_ref
  3.4 205.6 %shard_map.77 = (f32[1024,256]{1,0:T(8,128)}, f32[2,512,256]{2,1,0:T(8,128)}) custom-call(f32[2,1024,512]{2,1,0:T(8,128)} %ci_hbm.1, f32[2,512,256]{2,1,0:T(8,128)} %crhs_ref.1, f32[2,128,1024]{2,1,0:T(8,128)} %cu_hbm.1, s32[2,1024]{1,0:T(2,128)} %get-tuple-element.3.trow_ref, s32[2,1024,1]{2,1,0:T(8,128)} %copy.8.tcol_ref, f32[2048,1024]{1,0:T(8,128)} %ri_hbm.1, ...), custom_call_target="tpu_custom_call" | custom-call | tf_op jit(solution)/shard_map/pallas_call | solution.py:394
  209.0 2.3 %copy.30 = f32[1024,256]{1,0:T(8,128)} copy(f32[1024,256]{1,0:T(8,128)} %get-tuple-element.22) | data formatting | bytes 2097152
  211.3 2.3 %copy.31 = f32[2,512,256]{2,1,0:T(8,128)} copy(f32[2,512,256]{2,1,0:T(8,128)} %get-tuple-element.23) | data formatting | bytes 2097152
  (10 shorter events, 0.1 us)

commit v2 on v1

v2 whole, which is shorter than its diff:
```python
import functools

import jax
import jax.numpy as jnp
from jax import lax
from jax.experimental import pallas as pl
from jax.experimental.pallas import tpu as pltpu
from jax.sharding import PartitionSpec as P

MESH = pl.DeviceIdType.MESH
CHUNKS = 2
OFFSET = 1
GROUP = 1
PIECES = 4
f32, bf16 = jnp.float32, jnp.bfloat16


def split(x):
    high = x.astype(bf16)
    return high, (x - high.astype(f32)).astype(bf16)


def bit_orders(bits):
    rest = list(range(1, bits))
    if GROUP == 1:
        return ([(0,)] + [(b,) for b in rest], [(0,)] + [(b,) for b in rest[::-1]])
    groups = [(0,)] + [tuple(rest[i:i + GROUP]) for i in range(0, len(rest), GROUP)]
    return (groups, groups)


def block_position(block, order):
    position = 0
    for group in order:
        for bit in group:
            position = position * 2 + (block // (1 << bit)) % 2
    return position


def dot(a, b):
    return jnp.dot(a, b, preferred_element_type=f32)


def kernel(
    nb, nr, dims,
    ci_hbm, crhs_ref, cu_hbm, trow_ref, tcol_ref, ri_hbm, rrhs_ref,
    root_out, child_out,
    ci, cu, ri,
    part, fcr, fc, ug, frp, frr, fr, rep, repr_, cp, cpr,
    up, upx, bk, bkx, cb, cbx,
    rhs_w, tmp_t,
    load_sem, ar_s, ar_r, ch_s, ch_r,
):
    orders = bit_orders(nb.bit_length() - 1)
    me = lax.axis_index("bulk")
    row = lax.axis_index("row")
    C = fc.shape[-1]
    cols_a, cols_b, own, rows_a, nl = dims

    loads = [
        pltpu.make_async_copy(ci_hbm, ci, load_sem.at[0]),
        pltpu.make_async_copy(cu_hbm, cu, load_sem.at[1]),
        pltpu.make_async_copy(ri_hbm, ri, load_sem.at[2]),
    ]
    for load in loads:
        load.start()

    def bit_of(bit):
        return (me // (1 << bit)) % 2

    def peers(group, part):
        here = 0
        for bit in group:
            here = here * 2 + bit_of(bit)
        found = []
        for mask in range(1, 1 << len(group)):
            index, there = me, 0
            for k, bit in enumerate(group):
                mine = bit_of(bit)
                if (mask >> k) & 1:
                    index = index + (1 << bit) * (1 - 2 * mine)
                    mine = 1 - mine
                there = there * 2 + mine
            found.append((index, there * part))
        return here * part, found

    right = lax.rem(row + 1, nr)
    left = lax.rem(row + nr - 1, nr)
    barrier = pltpu.get_barrier_semaphore()
    greeted = 0
    for group in orders[0]:
        for index, _ in peers(group, 1)[1]:
            pl.semaphore_signal(barrier, inc=1, device_id={"bulk": index}, device_id_type=MESH)
            greeted += 1

    for side in (left, right):
        pl.semaphore_signal(barrier, inc=1, device_id={"row": side}, device_id_type=MESH)
    pl.semaphore_wait(barrier, greeted + 2)

    def remote(src, dst, send, recv, **where):
        return pltpu.make_async_remote_copy(
            src_ref=src, dst_ref=dst, send_sem=send, recv_sem=recv, device_id=where, device_id_type=MESH
        )

    pending = [[] for _ in range(CHUNKS)]

    def flush(h):
        for finish in pending[h]:
            finish()
        pending[h] = []

    def reduce_scatter(h, which, buf, rbuf, starts, out, produce):
        length, off, sends = buf.shape[2], 0, []
        for step in range(len(orders[0])):
            flights = []
            for f in range(2):
                if step == 0:
                    produce(f)
                group = orders[f][step]
                part = length >> len(group)
                here, others = peers(group, part)
                arrivals = []
                for m, (index, there) in enumerate(others):
                    copy = remote(
                        buf.at[h, f, pl.ds(pl.multiple_of(starts[f] + there, part), part)],
                        rbuf.at[h, f, pl.ds(off + m * part, part)],
                        ar_s.at[h, which, f, step, m], ar_r.at[h, which, f, step, m], bulk=index,
                    )
                    copy.start()
                    arrivals.append((copy, off + m * part))
                flights.append((pl.multiple_of(starts[f] + here, part), part, arrivals))
            yield
            if step == 0:
                flush(h)
            for f, (keep, part, arrivals) in enumerate(flights):
                total = buf[h, f, pl.ds(keep, part)]
                for copy, at in arrivals:
                    copy.wait_recv()
                    total = total + rbuf[h, f, pl.ds(at, part)]
                    sends.append(copy.wait_send)
                target = out if step == len(orders[0]) - 1 else buf
                target[h, f, pl.ds(keep, part)] = total
                starts[f] = keep
            off += length - part
            length = part
        pending[h] += sends

    def all_gather(h, which, buf, starts):
        sends, length = [], buf.shape[2] // nb
        for step in reversed(range(len(orders[0]))):
            flights = []
            for f in range(2):
                group = orders[f][step]
                here, others = peers(group, length)
                at = buf.at[h, f, pl.ds(pl.multiple_of(starts[f], length), length)]
                for m, (index, _) in enumerate(others):
                    copy = remote(at, at, ar_s.at[h, which, f, step, m], ar_r.at[h, which, f, step, m], bulk=index)
                    copy.start()
                    flights.append(copy)
                starts[f] = starts[f] - here
            yield
            if not sends:
                flush(h)
            for copy in flights:
                copy.wait_recv()
                sends.append(copy.wait_send)
            length = length << len(group)
        pending[h] += sends

    def chain(h, which, p, x, produce=None, stride=1):
        pieces = p.shape[1]

        @pl.when(row == 0)
        def _():
            x[h, 0] = jnp.zeros(x.shape[2:], f32)

        @pl.when(row == nr - 1)
        def _():
            x[h, 1] = jnp.zeros(x.shape[2:], f32)

        def flow(side, i, has_source, has_target, target):
            copy = remote(
                x.at[h, 2 + side, i], x.at[h, side, i],
                ch_s.at[h, which, side, i], ch_r.at[h, which, side, i], row=target,
            )

            @pl.when(has_source)
            def _():
                copy.wait_recv()

            @pl.when(has_target)
            def _():
                x[h, 2 + side, i] = x[h, side, i] + p[h, i]
                copy.start()

        for t in range(pieces + nr - 1):
            if t > 0:
                yield
            if t == 1:
                flush(h)
            if produce is not None and t < pieces and t % stride == 0:
                produce(t // stride)
            i = t - row

            @pl.when((i >= 0) & (i < pieces))
            def _():
                flow(0, i, row > 0, row < nr - 1, right)

            k = t - (nr - 1 - row)

            @pl.when((k >= 0) & (k < pieces))
            def _():
                flow(1, k, row < nr - 1, row > 0, left)

        def finish():
            for i in range(pieces):
                for side, has_target, target in ((0, row < nr - 1, right), (1, row > 0, left)):
                    @pl.when(has_target)
                    def _():
                        remote(
                            x.at[h, 2 + side, i], x.at[h, side, i],
                            ch_s.at[h, which, side, i], ch_r.at[h, which, side, i], row=target,
                        ).wait_send()

        pending[h].append(finish)

    def times(a_tile, count, store, h, width):
        def body(i, carry):
            high, low = split(a_tile(i))
            both = dot(high, rhs_w[h, :width]) + dot(low, rhs_w[h, :width])
            store(i, both[:, :C] + both[:, C:])
            return carry

        lax.fori_loop(0, count, body, 0)

    def keep_right(h, at, value):
        high, low = split(value)
        rhs_w[h, at, :C] = high
        rhs_w[h, at, C:] = low

    def keep_transposed(h, depth, k_tile, y_tile):
        for k in range(depth // k_tile):
            high, low = split(y_tile(k).T)
            tmp_t[h, :C, k * k_tile:(k + 1) * k_tile] = high
            tmp_t[h, C:, k * k_tile:(k + 1) * k_tile] = low

    def transposed_tile(a_tile, depth, k_tile, width, h):
        total = jnp.zeros((2 * C, width), f32)
        for k in range(depth // k_tile):
            high, low = split(a_tile(k))
            y = tmp_t[h, :, k * k_tile:(k + 1) * k_tile]
            total += dot(y, high) + dot(y, low)
        return (total[:C] + total[C:]).T

    def tiles(n, most):
        size = min(n, most)
        return size, n // size

    def program(h):
        lanes = slice(h * C, (h + 1) * C)
        if h == 0:
            loads[0].wait()
        tm, count = tiles(cols_a, 256)
        def produce1(j):
            keep_right(h, slice(0, cols_b), crhs_ref[j, :, lanes])

            def store(i, value):
                part[h, j, pl.ds(pl.multiple_of(i * tm, tm), tm)] = value

            times(lambda i: ci[j, pl.ds(pl.multiple_of(i * tm, tm), tm), :], count, store, h, cols_b)

        starts = [0, 0]
        yield from reduce_scatter(h, 0, part, fcr, starts, fc, produce1)
        yield from all_gather(h, 1, fc, starts)
        if h == 0:
            loads[1].wait()
        for j in range(2):
            keep_right(h, slice(0, cols_a), fc[h, j])

            def store(i, value, j=j):
                up[h, j] = value

            times(lambda i, j=j: cu[j], 1, store, h, cols_a)
        yield from chain(h, 0, up, upx)
        starts = []
        for j in range(2):
            position = block_position(me, orders[j])
            start = pl.multiple_of(position * nl, nl)
            starts.append(start)
            ug[h, j, pl.ds(start, nl)] = upx[h, 0, j] + up[h, j] + upx[h, 1, j]
        yield from all_gather(h, 2, ug, starts)
        tm, count = tiles(own, 256)
        nu = nb * nl
        kt, kcount = tiles(nu, 512)

        def assemble(i, carry):
            ids = lax.broadcasted_iota(jnp.int32, (tm, kt), 0) + (me * own + i * tm)
            at = pl.ds(pl.multiple_of(i * tm, tm), tm)
            total = jnp.zeros((tm, C), f32)
            for j in range(2):
                for k in range(kcount):
                    ks = slice(k * kt, (k + 1) * kt)
                    hit = jnp.where(ids == trow_ref[j:j + 1, ks], 1.0, 0.0).astype(bf16)
                    high, low = split(ug[h, j, ks])
                    total += dot(hit, high) + dot(hit, low)
            value = rrhs_ref[at, lanes] - total
            high, low = split(value)
            rhs_w[h, at, :C] = high
            rhs_w[h, at, C:] = low
            return carry

        lax.fori_loop(0, count, assemble, 0)
        if h == 0:
            loads[2].wait()
        per = rows_a // 2
        tm4, count4 = tiles(per, 256)

        def produce4(f):
            def store(i, value):
                frp[h, f, pl.ds(pl.multiple_of(i * tm4, tm4), tm4)] = value

            times(
                lambda i: ri[pl.ds(pl.multiple_of(f * per + i * tm4, tm4), tm4), :],
                count4, store, h, own,
            )

        starts = [0, 0]
        yield from reduce_scatter(h, 3, frp, frr, starts, fr, produce4)
        yield from all_gather(h, 4, fr, starts)
        pieces, size = bk.shape[1], bk.shape[2]
        width = min(256, own)
        kt5, _ = tiles(per, 512)
        halves = per // kt5

        keep_transposed(h, rows_a, kt5, lambda k: fr[h, k // halves, (k % halves) * kt5:(k % halves + 1) * kt5])

        def produce5(i):
            value = transposed_tile(
                lambda k: ri[k * kt5:(k + 1) * kt5, i * width:(i + 1) * width], rows_a, kt5, width, h
            )
            for n in range(width // size):
                bk[h, i * (width // size) + n] = value[n * size:(n + 1) * size]

        yield from chain(h, 1, bk, bkx, produce5, width // size)
        for i in range(pieces):
            value = bkx[h, 0, i] + bk[h, i] + bkx[h, 1, i]
            root_out[i * size:(i + 1) * size, lanes] = value
            keep_right(h, slice(i * size, (i + 1) * size), value)
        tm6, count6 = tiles(nu, 256)

        def produce6(j):
            def fetch(i, carry):
                at = pl.ds(pl.multiple_of(i * tm6, tm6), tm6)
                ids = lax.broadcasted_iota(jnp.int32, (tm6, own), 1) + me * own
                hit = jnp.where(ids == tcol_ref[j, at], 1.0, 0.0).astype(bf16)
                both = dot(hit, rhs_w[h, :own])
                rep[h, j, at] = both[:, :C] + both[:, C:]
                return carry

            lax.fori_loop(0, count6, fetch, 0)

        starts = [0, 0]
        yield from reduce_scatter(h, 5, rep, repr_, starts, rep, produce6)
        w7, count7 = tiles(cols_a, 256)

        def produce7(j):
            keep_transposed(h, nl, nl, lambda k: rep[h, j, pl.ds(starts[j], nl)])

            def body(i, carry):
                at = pl.ds(pl.multiple_of(i * w7, w7), w7)
                cp[h, j, at] = transposed_tile(lambda k: cu[j, :, at], nl, nl, w7, h)
                return carry

            lax.fori_loop(0, count7, body, 0)

        starts7 = [0, 0]
        yield from reduce_scatter(h, 6, cp, cpr, starts7, part, produce7)
        yield from all_gather(h, 7, part, starts7)
        pieces8, size8 = cb.shape[1], cb.shape[2]
        w8, count8 = tiles(cols_b, 256)
        kt8, _ = tiles(cols_a, 512)

        def produce8(n):
            j, i = n // count8, n % count8
            if i == 0:
                keep_transposed(
                    h, cols_a, kt8,
                    lambda k: fc[h, j, k * kt8:(k + 1) * kt8] - part[h, j, k * kt8:(k + 1) * kt8],
                )
            value = transposed_tile(
                lambda k: ci[j, k * kt8:(k + 1) * kt8, i * w8:(i + 1) * w8], cols_a, kt8, w8, h
            )
            for m in range(w8 // size8):
                cb[h, n * (w8 // size8) + m] = value[m * size8:(m + 1) * size8]

        yield from chain(h, 2, cb, cbx, produce8, w8 // size8)
        for i in range(pieces8):
            j, k = i // (pieces8 // 2), i % (pieces8 // 2)
            child_out[j, k * size8:(k + 1) * size8, lanes] = cbx[h, 0, i] + cb[h, i] + cbx[h, 1, i]

    running = [program(h) for h in range(CHUNKS)]
    turn = 0
    while any(p is not None for p in running):
        for h in range(CHUNKS):
            if running[h] is not None and turn >= h * OFFSET:
                try:
                    next(running[h])
                except StopIteration:
                    flush(h)
                    running[h] = None
        turn += 1


def per_device(nb, nr, child_inverse, child_rhs, child_update, targets, root_inverse, root_rhs):
    orders = bit_orders(nb.bit_length() - 1)
    _, cols_a, cols_b = child_inverse.shape
    nl = child_update.shape[1]
    rows_a, own = root_inverse.shape
    R = root_rhs.shape[1]
    H, C = CHUNKS, R // CHUNKS
    nu = nb * nl
    blocks = targets.reshape(2, nb, nl)
    placed = []
    for j in range(2):
        source = [0] * nb
        for block in range(nb):
            source[block_position(block, orders[j])] = block
        placed.append(jnp.concatenate([blocks[j, s] for s in source]))
    trow = jnp.stack(placed)
    tcol = trow[:, :, None]
    root_pieces = min(PIECES, own // 32)
    child_pieces = 2 * min(PIECES // 2, cols_b // 32)
    most = max(root_pieces, child_pieces, 2)
    any_, vmem = pl.BlockSpec(memory_space=pl.ANY), pl.BlockSpec(memory_space=pltpu.VMEM)

    def sums(n, count=2):
        return [pltpu.VMEM((H, 2, n, C), f32)] * count

    def chains(pieces, rows):
        return [pltpu.VMEM((H, pieces, rows, C), f32), pltpu.VMEM((H, 4, pieces, rows, C), f32)]

    return pl.pallas_call(
        functools.partial(kernel, nb, nr, (cols_a, cols_b, own, rows_a, nl)),
        out_shape=(
            jax.ShapeDtypeStruct(root_rhs.shape, f32),
            jax.ShapeDtypeStruct(child_rhs.shape, f32),
        ),
        in_specs=[any_, vmem, any_, vmem, vmem, any_, vmem],
        out_specs=(vmem, vmem),
        scratch_shapes=[
            pltpu.VMEM(child_inverse.shape, f32),
            pltpu.VMEM(child_update.shape, f32),
            pltpu.VMEM(root_inverse.shape, f32),
            *sums(cols_a, 3),
            pltpu.VMEM((H, 2, nu, C), f32),
            *sums(rows_a // 2, 3),
            *sums(nu),
            *sums(cols_a),
            *chains(2, nl),
            *chains(root_pieces, own // root_pieces),
            *chains(child_pieces, 2 * cols_b // child_pieces),
            pltpu.VMEM((H, max(own, cols_a, cols_b), 2 * C), bf16),
            pltpu.VMEM((H, 2 * C, max(rows_a, cols_a, nl)), bf16),
            pltpu.SemaphoreType.DMA((3,)),
            pltpu.SemaphoreType.DMA((H, 8, 2, len(orders[0]), (1 << GROUP) - 1)),
            pltpu.SemaphoreType.DMA((H, 8, 2, len(orders[0]), (1 << GROUP) - 1)),
            pltpu.SemaphoreType.DMA((H, 3, 2, most)),
            pltpu.SemaphoreType.DMA((H, 3, 2, most)),
        ],
        compiler_params=pltpu.CompilerParams(
            collective_id=0, has_side_effects=True, vmem_limit_bytes=62 * 1024 * 1024
        ),
    )(child_inverse, child_rhs, child_update, trow, tcol, root_inverse, root_rhs)


def solution(mesh):
    return jax.shard_map(
        functools.partial(per_device, mesh.shape["bulk"], mesh.shape["row"]),
        mesh=mesh,
        in_specs=(
            P(None, "row", "bulk"),
            P(None, "bulk", None),
            P(None, "bulk", "row"),
            P(),
            P("row", "bulk"),
            P("bulk", None),
        ),
        out_specs=(P("bulk", None), P(None, "bulk", None)),
        check_vma=False,
    )
```

time: 214 us -> 200 us (0.935)
  Pallas kernels: 206 us -> 192 us
    pallas_call x1, Pallas kernels: 206 us -> 192 us  [per_device(): pl.pallas_call(functools.partial(kernel, nb, nr, (cols_a, cols_b, own, ro...]
where the time goes in v2:
time: 200 us
  Pallas kernels  192 us (96%)
  local copies, waits for them, and re-layouts  6.63 us (3%)
    pallas_call x1, Pallas kernels, per_device(): pl.pallas_call(functools.partial(kernel, nb, nr, (cols_a, cols_b, own, ro...  192 us
    unnamed x10, local copies, waits for them, and re-layouts  5.28 us

profile of v2, /device:TPU:0, one launch (start us, length us, event | category | flops | bytes accessed | tf_op | source)
XLA Modules:
  0.0 200.1 jit_solution(1511766478459004056)
XLA Ops:
  0.6 0.7 copy.11
  1.5 0.6 fusion
  2.1 1.3 copy.8.tcol_ref
  3.4 192.1 %shard_map.77 = (f32[1024,256]{1,0:T(8,128)}, f32[2,512,256]{2,1,0:T(8,128)}) custom-call(f32[2,1024,512]{2,1,0:T(8,128)} %ci_hbm.1, f32[2,512,256]{2,1,0:T(8,128)} %crhs_ref.1, f32[2,128,1024]{2,1,0:T(8,128)} %cu_hbm.1, s32[2,1024]{1,0:T(2,128)} %get-tuple-element.3.trow_ref, s32[2,1024,1]{2,1,0:T(8,128)} %copy.8.tcol_ref, f32[2048,1024]{1,0:T(8,128)} %ri_hbm.1, ...), custom_call_target="tpu_custom_call" | custom-call | tf_op jit(solution)/shard_map/pallas_call | solution.py:441
  195.6 2.3 %copy.30 = f32[1024,256]{1,0:T(8,128)} copy(f32[1024,256]{1,0:T(8,128)} %get-tuple-element.22) | data formatting | bytes 2097152
  197.8 2.3 %copy.31 = f32[2,512,256]{2,1,0:T(8,128)} copy(f32[2,512,256]{2,1,0:T(8,128)} %get-tuple-element.23) | data formatting | bytes 2097152
  (10 shorter events, 0.1 us)
